TPU v7x, 32 devices: a whole 2x2x4 slice. The times are simulated.
32 devices in a mesh: pipe: 4 (over x, core), tensor: 2 (over y), dp: 4 (over z).
Axes of the slice: x: 2, y: 2, z: 4, core: 2. Of those that a mesh axis runs over, the one named last changes fastest.
Arguments:
- inputs: bfloat16 [2, 256, 4096], P(None, 'dp'), may hold values from -6 to 6
- layer_gain: float32 [4, 4096], P('pipe'), may hold values from 0.5 to 1.5
- up_weight: bfloat16 [4, 4096, 14336], P('pipe', 'dp', 'tensor'), may hold values from -0.09375 to 0.09375
- down_weight: bfloat16 [4, 14336, 4096], P('pipe', 'tensor', 'dp'), may hold values from -0.046875 to 0.046875
- final_gain: float32 [4096], replicated, may hold values from 0.5 to 1.5
- value_head: bfloat16 [4096], replicated, may hold values from -6 to 6
- q_head: bfloat16 [4096, 65536], P(None, ('pipe', 'tensor', 'dp')), may hold values from -620 to 620
- target_head: bfloat16 [4096, 65536], P(None, ('pipe', 'tensor', 'dp')), may hold values from -18 to 18
- actions: int32 [2, 256], replicated, may hold values from 0 to 65535
- rewards: int32 [2, 256], replicated, may hold values from -2 to 2
- done: int32 [2, 256], replicated, may hold values 0 or 1
- order: int32 [2], replicated, may hold values from 0 to 1, each once
Outputs:
- state_values: float32 [2, 256], replicated
- advantages: float32 [2, 256], replicated
- td_errors: float32 [2, 256], replicated
- value_loss: float32 [], replicated
- q_loss: float32 [], replicated
- lse_grad: bfloat16 [4096, 65536], P(None, ('pipe', 'tensor', 'dp'))
Inputs may be any that keep to these rules, and one draw needn't show every extreme that they name: `order`: each micro-batch once.
All inputs are finite; a program needn't handle non-finite values.
Results may differ from a plain program's by a relative error of at most 0.04.
Values may be sent and summed in bfloat16 or wider, within the bound.
No kernel may reach another device: no remote copies, remote signals or barrier semaphores. Data moves between devices by JAX's collectives and lax.ppermute only.
A program may use at most 256 MiB of HBM per device.

v0:
```python
import jax
import jax.numpy as jnp
from jax import lax
from jax.sharding import PartitionSpec as P

VQ = 65536


EPS = 1e-05
GAMMA = 0.99
TAU = 0.7
ALPHA = 0.5


def from_behind(block, axis, distance):
    devices = range(lax.axis_size(axis))
    route = [(i - distance, i) for i in devices if i - distance in devices]
    return lax.ppermute(block, axis, route)


def spread(value, axis, source):
    kept = jnp.where(lax.axis_index(axis) == source, value, 0).astype(value.dtype)
    return lax.psum(kept, axis)


def merged(part, axis, combine):
    gathered = jax.tree.map(lambda a: lax.all_gather(a, axis), part)

    def take(source):
        return jax.tree.map(lambda a: lax.dynamic_index_in_dim(a, source, 0, False), gathered)

    return lax.fori_loop(
        1, lax.axis_size(axis), lambda source, state: combine(state, take(source)), take(0)
    )


def normed(values, gain):
    wide = values.astype(jnp.float32)
    factor = lax.rsqrt(jnp.mean(wide * wide, axis=-1, keepdims=True) + EPS)
    return wide * factor * gain


def combine_totals(first, second):
    highest = jnp.maximum(first[0], second[0])
    summed = first[1] * jnp.exp(first[0] - highest) + second[1] * jnp.exp(second[0] - highest)
    return (highest, summed)


def local(
    inputs,
    layer_gain,
    up_weight,
    down_weight,
    final_gain,
    value_head,
    q_head,
    target_head,
    actions,
    rewards,
    done,
    order,
):
    section = lax.axis_index("pipe")
    sections = lax.axis_size("pipe")
    tensor_size = lax.axis_size("tensor")
    micro = inputs.shape[0]
    window = inputs.shape[1]
    width_model = inputs.shape[2]
    chosen = jnp.take(inputs, order, axis=0)
    gain = layer_gain[0]
    local_weights = (up_weight[0], down_weight[0])
    held = (
        lax.all_gather(local_weights[0], "dp", axis=0, tiled=True),
        lax.all_gather(local_weights[1], "dp", axis=1, tiled=True),
    )
    share = window // tensor_size
    chosen = lax.dynamic_slice_in_dim(chosen, lax.axis_index("tensor") * share, share, 1)
    piece_rows = chosen.shape[1]

    def forward(states, weights):
        w_up, w_down = weights
        normal = normed(states, gain).astype(jnp.bfloat16)
        upper = jnp.dot(
            lax.all_gather(normal, "tensor", axis=0, tiled=True),
            w_up,
            preferred_element_type=jnp.float32,
        )
        hidden = jax.nn.silu(upper).astype(jnp.bfloat16)
        summed = lax.psum_scatter(
            jnp.dot(hidden, w_down, preferred_element_type=jnp.float32),
            "tensor",
            scatter_dimension=0,
            tiled=True,
        )
        return (states.astype(jnp.float32) + summed).astype(jnp.bfloat16)

    def advance(step_index, carry):
        arriving, stored = carry
        first = lax.dynamic_index_in_dim(
            chosen, jnp.minimum(step_index, micro - 1), 0, keepdims=False
        )
        entering = jnp.where(section == 0, first, arriving)
        leaving = forward(entering, held)
        slot = step_index - (sections - 1)
        keeping = (slot >= 0) & (section == sections - 1)
        updated = lax.dynamic_update_index_in_dim(stored, leaving, jnp.clip(slot, 0, micro - 1), 0)
        stored = jnp.where(keeping, updated, stored)
        arriving = from_behind(leaving, "pipe", 1)
        return (arriving, stored)

    initial = (
        jnp.zeros((piece_rows, width_model), jnp.bfloat16),
        jnp.zeros((micro, piece_rows, width_model), jnp.bfloat16),
    )
    arriving, stored = lax.fori_loop(0, micro + sections - 1, advance, initial)
    final_rows = spread(stored, "pipe", sections - 1)
    normal_final = normed(final_rows, final_gain).astype(jnp.bfloat16)
    normal_final = lax.all_gather(normal_final, "tensor", axis=1, tiled=True)
    everyone = lax.all_gather(normal_final, "dp", axis=1, tiled=True)
    flat = everyone.reshape(-1, width_model)
    count = flat.shape[0]
    factor = width_model ** (-0.5)
    columns_here = q_head.shape[1]
    offset = lax.axis_index(("pipe", "tensor", "dp")) * columns_here
    action = jnp.take(actions, order, axis=0).reshape(-1)
    reward = jnp.take(rewards, order, axis=0).reshape(-1).astype(jnp.float32)
    finished = jnp.take(done, order, axis=0).reshape(-1).astype(jnp.float32)
    values = jnp.dot(flat, value_head, preferred_element_type=jnp.float32) * factor
    logits = jnp.dot(flat, q_head, preferred_element_type=jnp.float32) * factor
    onehot = (
        action[:, None] == offset + lax.broadcasted_iota(jnp.int32, (1, columns_here), 1)
    ).astype(jnp.float32)
    local_top = jnp.max(logits, axis=-1)
    local_total = jnp.sum(jnp.exp(logits - local_top[:, None]), axis=-1)
    taken_part = jnp.sum(logits * onehot, axis=-1)
    owned = (action >= offset) & (action < offset + columns_here)
    local_index = jnp.clip(action - offset, 0, columns_here - 1)
    target_cols = jnp.take(target_head, local_index, axis=1)
    target_dot = (
        jnp.einsum("nd,dn->n", flat, target_cols, preferred_element_type=jnp.float32) * factor
    )
    target_part = jnp.where(owned, target_dot, 0.0)
    highest, summed = merged((local_top, local_total), ("pipe", "tensor", "dp"), combine_totals)
    taken, target_taken = lax.psum((taken_part, target_part), ("pipe", "tensor", "dp"))
    lse = highest + jnp.log(summed)
    windows = values.reshape(-1, window)
    following = jnp.concatenate(
        [windows[:, 1:], jnp.zeros((windows.shape[0], 1), jnp.float32)], axis=1
    ).reshape(-1)
    bootstrap = 0.5 * reward + GAMMA * (1.0 - finished) * following
    td_value = taken - bootstrap
    advantage = target_taken - values
    weight = jnp.where(advantage < 0, 1.0 - TAU, TAU)
    value_loss = jnp.mean(weight * advantage * advantage)
    q_loss = jnp.mean(td_value * td_value + ALPHA * (lse - taken))
    probs = jnp.exp(logits - lse[:, None]).astype(jnp.bfloat16)
    scale = VQ * factor / count
    gathered_sum = lax.dot_general(
        flat, probs, (((0,), (0,)), ((), ())), preferred_element_type=jnp.float32
    )
    lse_grad = (gathered_sum * scale).astype(jnp.bfloat16)
    shape = (micro, count // micro)
    return (
        values.reshape(shape),
        advantage.reshape(shape),
        td_value.reshape(shape),
        value_loss,
        q_loss,
        lse_grad,
    )


def solution(mesh):
    in_specs = (
        P(None, "dp", None),
        P("pipe", None),
        P("pipe", "dp", "tensor"),
        P("pipe", "tensor", "dp"),
        P(),
        P(),
        P(None, ("pipe", "tensor", "dp")),
        P(None, ("pipe", "tensor", "dp")),
        P(),
        P(),
        P(),
        P(),
    )
    out_specs = (P(), P(), P(), P(), P(), P(None, ("pipe", "tensor", "dp")))
    return jax.shard_map(local, mesh=mesh, in_specs=in_specs, out_specs=out_specs, check_vma=False)
```

profile of v0, /device:TPU:0, one launch (start us, length us, event | category | flops | bytes accessed | tf_op | source)
XLA Modules:
  0.0 2725.8 jit_solution(8402949604991874543)
XLA Ops:
  7.2 0.7 all-gather.15.cloned.1.call-update
  8.0 0.7 all-gather.17.cloned.1.call-update
  8.8 0.6 gather_fusion
  9.6 977.1 %all-gather.15.cloned.1.call-done = bf16[1,4096,7168]{2,1,0:T(8,128)(2,1)} async-done(((bf16[1,1024,7168]{2,1,0:T(8,128)(2,1)}), bf16[1,4096,7168]{2,1,0:T(8,128)(2,1)}) %all-gather.15.cloned.1.call-update) | async-done | bytes 58720272 | tf_op jit(solution)/shard_map/all_gather | solution.py:73
  986.7 974.2 %all-gather.17.cloned.1.call-done = bf16[1,7168,4096]{2,1,0:T(8,128)(2,1)} async-done(((bf16[1,7168,1024]{2,1,0:T(8,128)(2,1)}), bf16[1,7168,4096]{2,1,0:T(8,128)(2,1)}) %all-gather.17.cloned.1.call-update) | async-done | bytes 58720272 | tf_op jit(solution)/shard_map/all_gather | solution.py:74
  1961.0 397.3 %while.34 = (s32[]{:T(128)}, bf16[32,4096]{1,0:T(8,128)(2,1)S(1)}, bf16[2,32,4096]{2,1,0:T(8,128)(2,1)S(1)}, pred[]{:T(512)}, bf16[2,32,4096]{2,1,0:T(8,128)(2,1...) while((s32[]{:T(128)}, bf16[32,4096]{1,0:T(8,128)(2,1)S(1)}, ...), condition=%wide.region_3.4_spmd, body=%wide.region_0.3_spmd.sunk | while | flops 7520059392 | bytes 130302776 | solution.py:115
  1961.4 8.9 all_gather.43
  1970.3 21.1 multiply_convert_fusion.7
  1991.4 22.5 fusion.57
  2014.0 18.7 reduce-scatter.2.cloned.1.call-done
  2032.6 1.1 fusion.58
  2033.8 1.6 collective-permute-start
  2035.4 1.1 collective-permute-done
  2036.9 7.0 all_gather.43
  2043.9 21.1 multiply_convert_fusion.7
  2065.0 22.5 fusion.57
  2087.6 25.5 reduce-scatter.2.cloned.1.call-done
  2113.1 1.1 fusion.58
  2114.2 1.6 collective-permute-start
  2115.8 1.1 collective-permute-done
  2117.3 7.0 all_gather.43
  2124.4 21.1 multiply_convert_fusion.7
  2145.5 22.5 fusion.57
  2168.0 25.5 reduce-scatter.2.cloned.1.call-done
  2193.5 1.1 fusion.58
  2194.7 1.6 collective-permute-start
  2196.3 1.1 collective-permute-done
  2197.8 7.0 all_gather.43
  2204.8 21.1 multiply_convert_fusion.7
  2225.9 22.5 fusion.57
  2248.5 25.5 reduce-scatter.2.cloned.1.call-done
  2274.0 1.1 fusion.58
  2275.1 1.6 collective-permute-start
  2276.7 1.1 collective-permute-done
  2278.2 7.0 all_gather.43
  2285.2 21.1 multiply_convert_fusion.7
  2306.4 22.5 fusion.57
  2328.9 25.5 reduce-scatter.2.cloned.1.call-done
  2354.4 1.1 fusion.58
  2355.5 1.6 collective-permute-start
  2357.2 1.1 collective-permute-done
  2358.3 0.8 broadcast_select_fusion
  2359.2 41.2 %all-reduce.4.cloned.1.call-done = bf16[2,32,4096]{2,1,0:T(8,128)(2,1)} async-done(((bf16[2,32,4096]{2,1,0:T(8,128)(2,1)}), bf16[2,32,4096]{2,1,0:T(8,128)(2,1)}) %all-reduce.4.cloned.1.call-update) | async-done | bytes 524304 | tf_op jit(solution)/shard_map/psum | solution.py:23
  2400.4 1.2 fusion.10
  2401.6 2.0 fusion.12
  2403.9 21.3 all-gather.11.cloned.1.call-done
  2425.3 0.7 gather_fusion.2
  2426.1 21.4 copy.19
  2447.5 0.7 gather_fusion.3
  2448.2 0.7 gather_fusion.4
  2449.0 16.6 gather_fusion.1
  2465.6 41.8 %all-gather.13.cloned.1.call-done = bf16[2,256,4096]{2,1,0:T(8,128)(2,1)} async-done(((bf16[2,64,4096]{2,1,0:T(8,128)(2,1)}), bf16[2,256,4096]{2,1,0:T(8,128)(2,1)}) %all-gather.13.cloned.1.call-update) | async-done | bytes 4194320 | tf_op jit(solution)/shard_map/all_gather | solution.py:119
  2507.4 13.1 fusion.23
  2520.6 1.1 exponential_reduce_fusion
  2521.7 66.1 %all-gather.5 = f32[32,1,512]{2,1,0:T(1,128)S(1)} all-gather(f32[1,1,512]{2,1,0:T(1,128)S(1)} %bitcast.92), channel_id=5, replica_groups=mesh['pipe'=4,'tensor'=2,'dp'=4] {'pipe','tensor','dp'}, dimensions={0}, use_global_device_ids=true | all-gather | bytes 67584 | tf_op jit(solution)/shard_map/all_gather | solution.py:27
  2587.9 63.9 %all-gather.4 = f32[32,1,512]{2,1,0:T(1,128)S(1)} all-gather(f32[1,1,512]{2,1,0:T(1,128)S(1)} %bitcast.91), channel_id=4, replica_groups=mesh['pipe'=4,'tensor'=2,'dp'=4] {'pipe','tensor','dp'}, dimensions={0}, use_global_device_ids=true | all-gather | bytes 67584 | tf_op jit(solution)/shard_map/all_gather | solution.py:27
  2651.8 1.2 fusion.26
  2653.0 1.7 fusion.8
  2654.6 40.1 %all-reduce.1 = (f32[512]{0:T(512)S(1)}, f32[512]{0:T(512)S(1)}) all-reduce(f32[512]{0:T(512)S(1)} %multiply_select_fusion, f32[512]{0:T(512)S(1)} %get-tuple-element.349), channel_id=1, replica_groups=mesh['pipe'=4,'tensor'=2,'dp'=4] {'pipe','tensor','dp'}, use_global_device_ids=true, to_apply=%region_6.8 | all-reduce | flops 1024 | bytes 8192 | tf_op jit(solution)/shard_map/psum | solution.py:144
  2694.7 0.6 fusion.13
  2695.4 0.6 reshape.115
  2696.0 1.8 while.35
  2698.0 0.6 add_reduce_fusion
  2698.6 15.7 multiply_convert_fusion.2
  (154 shorter events, 5.3 us)
Async XLA Ops:
  7.2 1.6 copy-start
  7.2 979.5 %all-gather.15.cloned.1.call-start = ((), (), s32[]{:S(2)}) async-start(), calls=%async_computation.4 | async-start | bytes 73400320 | tf_op jit(solution)/shard_map/all_gather | solution.py:73
  7.9 0.8 copy-start.14
  7.9 1953.0 %copy-start.5 = (f32[1,4096]{1,0:T(1,128)S(1)}, f32[1,4096]{1,0:T(1,128)}, u32[]{:S(2)}) copy-start(f32[1,4096]{1,0:T(1,128)} %param.19) | copy-start | bytes 49156
  7.9 1953.0 %all-gather.17.cloned.1.call-start = ((), (), s32[]{:S(2)}) async-start(), calls=%async_computation.5 | async-start | bytes 73400320 | tf_op jit(solution)/shard_map/all_gather | solution.py:74
  8.7 1952.2 %copy-start.10 = (s32[1024]{0:T(1024)}, s32[1024]{0:T(1024)S(1)}, u32[]{:S(2)}) copy-start(s32[1024]{0:T(1024)S(1)} %pad_clamp_fusion.1) | copy-start | bytes 12292
  9.4 1951.5 %copy-start.12 = (pred[2]{0:T(512)(128)(4,1)}, pred[2]{0:T(512)(128)(4,1)S(1)}, u32[]{:S(2)}) copy-start(pred[2]{0:T(512)(128)(4,1)S(1)} %compare_and_fusion.1) | copy-start | bytes 10
  1961.0 440.6 %copy-start.9 = (f32[4096]{0:T(1024)S(1)}, f32[4096]{0:T(1024)}, u32[]{:S(2)}) copy-start(f32[4096]{0:T(1024)} %param.22) | copy-start | bytes 49156
  1961.0 71.6 %reduce-scatter.2.cloned.1.call-start = ((), (), s32[]{:S(2)}) async-start(), calls=%async_computation.6 | async-start | bytes 1572864 | tf_op jit(solution)/shard_map/while/body/eval_jaxpr/reduce_scatter | solution.py:89
  2033.8 2.7 collective-permute-start
  2036.5 76.5 %reduce-scatter.2.cloned.1.call-start = ((), (), s32[]{:S(2)}) async-start(), calls=%async_computation.6 | async-start | bytes 1572864 | tf_op jit(solution)/shard_map/while/body/eval_jaxpr/reduce_scatter | solution.py:89
  2114.2 2.7 collective-permute-start
  2117.0 76.6 %reduce-scatter.2.cloned.1.call-start = ((), (), s32[]{:S(2)}) async-start(), calls=%async_computation.6 | async-start | bytes 1572864 | tf_op jit(solution)/shard_map/while/body/eval_jaxpr/reduce_scatter | solution.py:89
  2194.7 2.7 collective-permute-start
  2197.4 76.5 %reduce-scatter.2.cloned.1.call-start = ((), (), s32[]{:S(2)}) async-start(), calls=%async_computation.6 | async-start | bytes 1572864 | tf_op jit(solution)/shard_map/while/body/eval_jaxpr/reduce_scatter | solution.py:89
  2275.1 2.7 collective-permute-start
  2277.8 76.5 %reduce-scatter.2.cloned.1.call-start = ((), (), s32[]{:S(2)}) async-start(), calls=%async_computation.6 | async-start | bytes 1572864 | tf_op jit(solution)/shard_map/while/body/eval_jaxpr/reduce_scatter | solution.py:89
  2355.5 2.7 collective-permute-start
  2358.3 67.0 %copy-start.6 = (s32[2,256]{1,0:T(2,128)S(1)}, s32[2,256]{1,0:T(2,128)}, u32[]{:S(2)}) copy-start(s32[2,256]{1,0:T(2,128)} %param.26) | copy-start | bytes 6148
  2358.3 67.7 %copy-start.13 = (pred[2]{0:T(512)(128)(4,1)S(1)}, pred[2]{0:T(512)(128)(4,1)}, u32[]{:S(2)}) copy-start(pred[2]{0:T(512)(128)(4,1)} %copy-done.12) | copy-start | bytes 10
  2358.3 42.1 %all-reduce.4.cloned.1.call-start = ((), (), s32[]{:S(2)}) async-start(), calls=%async_computation.1 | async-start | bytes 1048576 | tf_op jit(solution)/shard_map/psum | solution.py:23
  2359.1 66.1 %all-gather.11.cloned.1.call-start = ((), (), s32[]{:S(2)}) async-start(), calls=%async_computation.2 | async-start | bytes 1572864 | tf_op jit(solution)/shard_map/all_gather | solution.py:118
  2403.7 103.7 %all-gather.13.cloned.1.call-start = ((), (), s32[]{:S(2)}) async-start(), calls=%async_computation.3 | async-start | bytes 5242880 | tf_op jit(solution)/shard_map/all_gather | solution.py:119
  2426.1 21.4 copy-start.11
  2426.1 21.4 copy-start.7
  2426.1 22.1 copy-start.8
  2520.6 132.4 %copy-start.4 = (f32[512,2048]{1,0:T(8,128)}, f32[512,2048]{1,0:T(8,128)S(1)}, u32[]{:S(2)}) copy-start(f32[512,2048]{1,0:T(8,128)S(1)} %get-tuple-element.399) | copy-start | bytes 12582916
  2520.6 131.2 %copy-start.3 = (bf16[2,256,4096]{2,1,0:T(8,128)(2,1)S(1)}, bf16[2,256,4096]{2,1,0:T(8,128)(2,1)}, u32[]{:S(2)}) copy-start(bf16[2,256,4096]{2,1,0:T(8,128)(2,1)} %all-gather.13.cloned.1.call-done) | copy-start | bytes 12582916
  2520.6 132.4 %copy-start.2 = (bf16[512,4096]{1,0:T(8,128)(2,1)S(1)}, bf16[512,4096]{1,0:T(8,128)(2,1)}, u32[]{:S(2)}) copy-start(bf16[512,4096]{1,0:T(8,128)(2,1)} %gather_fusion.1) | copy-start | bytes 12582916
  2698.6 18.1 copy-start.1
Sparse Core Ops, SparseCore 0:
  9.6 977.0 all-gather.14
  988.3 972.5 all-gather.16
  2014.1 18.5 reduce-scatter.1
  2087.7 25.3 reduce-scatter.1
  2168.1 25.3 reduce-scatter.1
  2248.6 25.3 reduce-scatter.1
  2329.0 25.3 reduce-scatter.1
  2362.0 38.3 all-reduce.3
  2403.8 21.3 all-gather.10
  2426.6 80.7 all-gather.12
where the time goes:
time: 2730 us
  waiting for transfers between devices  2180 us (80%)
  matrix products  248 us (9%)
  blocking collectives  207 us (8%)
  local copies, waits for them, and re-layouts  43.2 us (2%)
    all_gather x1, waiting for transfers between devices, local(): lax.all_gather(local_weights[0], 'dp', axis=0, tiled=True)  977 us
    all_gather x1, waiting for transfers between devices, local(): lax.all_gather(local_weights[1], 'dp', axis=1, tiled=True)  974 us
    all_gather x2, blocking collectives, merged(): gathered = jax.tree.map(lambda a: lax.all_gather(a, axis), part)  130 us
    reduce_scatter x5, waiting for transfers between devices, forward(): lax.psum_scatter(jnp.dot(hidden, w_down, preferred_element_type=jnp.float...  121 us
    dot_general x5, matrix products, forward(): jnp.dot(hidden, w_down, preferred_element_type=jnp.float32)  113 us
    dot_general x5, matrix products, forward(): jnp.dot(lax.all_gather(normal, 'tensor', axis=0, tiled=True), w_up, prefe...  105 us
  transfers between devices with their start and end apart: 15, of which 15 were waited for; matrix products, arithmetic and copies ran while one was open for 2% of the time, Pallas kernels for 0%

commit v1 on v0

v1 whole, which is shorter than its diff:
```python
import jax
import jax.numpy as jnp
from jax import lax
from jax.sharding import PartitionSpec as P

VQ = 65536


EPS = 1e-05
GAMMA = 0.99
TAU = 0.7
ALPHA = 0.5

AXES = ("pipe", "tensor", "dp")


def send(block, pairs):
    _, tensors, dps = (lax.axis_size(a) for a in AXES)

    def flat(c):
        return (c[0] * tensors + c[1]) * dps + c[2]

    return lax.ppermute(block, AXES, [(flat(a), flat(b)) for a, b in pairs])


def along_dp(block, pipe, moves):
    pipes = [p for p in range(lax.axis_size("pipe")) if p % 2 == pipe % 2]
    rows = range(lax.axis_size("tensor"))
    pairs = [((p, t, a), (p, t, b)) for p in pipes for t in rows for a, b in moves]
    return send(block, pairs)


def over_cells(block, hops, across=False):
    tensors, dps = lax.axis_size("tensor"), lax.axis_size("dp")
    cells = [(t, d) for t in range(tensors) for d in range(dps)]
    flip = 1 if across else 0
    return send(block, [((a, t, d), (b, t ^ flip, d)) for a, b in hops for t, d in cells])


OUTER = ((0, 1), (3, 2))
OUTWARD = ((1, 0), (2, 3))
MIDDLE = ((1, 2), (2, 1))
SWAP = ((0, 1), (1, 0), (2, 3), (3, 2))
SKIP = ((0, 2), (2, 0), (1, 3), (3, 1))
MIRROR = ((0, 3), (3, 0), (1, 2), (2, 1))


def gathered(own, pipe):
    rank = lax.axis_index("dp")
    inner = (rank == 1) | (rank == 2)
    next1 = along_dp(own, pipe, SWAP)
    middle = along_dp(own, pipe, MIDDLE)
    next2_inner = along_dp(next1, pipe, MIDDLE)
    next2_outer = along_dp(middle, pipe, OUTWARD)
    next3_outer = along_dp(next2_inner, pipe, OUTWARD)
    next2 = jnp.where(inner, next2_inner, next2_outer)
    next3 = jnp.where(inner, middle, next3_outer)
    return own, next1, next2, next3


def hidden_layer(states, gain, w_up, w_down, pipe):
    rank = lax.axis_index("dp")
    size = lax.axis_size("dp")
    rows, width = states.shape
    block = w_up.shape[1] // size
    wide = states.astype(jnp.float32)
    scaled = (wide * gain).astype(jnp.bfloat16)
    squares = jnp.sum(wide * wide, axis=1)
    squares = squares + along_dp(squares, pipe, SWAP)
    squares = squares + along_dp(squares, pipe, SKIP)
    factor = lax.rsqrt(squares / (width * size) + EPS)[:, None]

    def part(flip):
        columns = lax.dynamic_slice_in_dim(w_up, (rank ^ flip) * block, block, 1)
        return jnp.dot(scaled, columns, preferred_element_type=jnp.float32)

    def lower(values):
        return values.astype(jnp.bfloat16)

    def add(values, other):
        return values + other.astype(jnp.float32)

    part3 = part(3)
    far = along_dp(lower(part3), pipe, OUTER)
    sum2 = lower(add(part(2), far))
    outer2 = along_dp(sum2, pipe, OUTER)
    middle2 = along_dp(sum2, pipe, MIDDLE)
    sum1 = lower(add(part(1), middle2))
    near = along_dp(sum1, pipe, SWAP)
    cross = along_dp(lower(add(part3, outer2)), pipe, MIDDLE)
    upper = add(add(part(0), near), cross) * factor
    own = lower(jax.nn.silu(upper))
    total = jnp.zeros((rows, width), jnp.float32)
    for flip, piece in enumerate(gathered(own, pipe)):
        weights = lax.dynamic_slice_in_dim(w_down, (rank ^ flip) * block, block, 0)
        total = total + jnp.dot(piece, weights, preferred_element_type=jnp.float32)
    return total


def first_states(chosen):
    rank = lax.axis_index("dp")
    size = lax.axis_size("dp")
    window, width = chosen.shape
    share = width // size
    states = jnp.zeros((size, window, share), chosen.dtype)
    for flip, moves in enumerate((None, SWAP, SKIP, MIRROR)):
        piece = lax.dynamic_slice_in_dim(chosen, (rank ^ flip) * share, share, 1)
        if flip:
            piece = along_dp(piece, 0, moves)
        states = lax.dynamic_update_slice_in_dim(states, piece[None], rank ^ flip, 0)
    return states.reshape(size * window, share)


def handed_on(states, total, hops):
    tensors = lax.axis_size("tensor")
    if tensors == 2:
        mine = lax.axis_index("tensor") == 0
        base = jnp.where(mine, states.astype(jnp.float32), 0.0)
        part = (base + total).astype(jnp.bfloat16)
        straight = over_cells(part, hops)
        across = over_cells(part, hops, across=True)
        return (straight.astype(jnp.float32) + across.astype(jnp.float32)).astype(jnp.bfloat16)
    whole = (states.astype(jnp.float32) + lax.psum(total, "tensor")).astype(jnp.bfloat16)
    return over_cells(whole, hops)


def next_hops(pipe, sections):
    if pipe % 2 == 0:
        return [(p, p + 1) for p in range(0, sections - 1, 2)]
    return [(pipe, pipe + 1)]


def final_states(states, total):
    sections = lax.axis_size("pipe")
    rank = lax.axis_index("dp")
    pipe = lax.axis_index("pipe")
    last = sections - 1
    done = handed_on(states, total, [(last, last - 1)])
    for target in range(0, last - 1, 2):
        moved = over_cells(done, [(last - 1, target)])
        done = jnp.where(pipe == target, moved, done)
    rows, share = done.shape
    size = lax.axis_size("dp")
    whole = jnp.zeros((rows, size * share), done.dtype)
    for flip, piece in enumerate(gathered(done, 0)):
        whole = lax.dynamic_update_slice_in_dim(whole, piece, (rank ^ flip) * share, 1)
    twin = over_cells(whole, [(p, p + 1) for p in range(0, sections - 1, 2)])
    return jnp.where(pipe % 2 == 0, whole, twin)


def merged_stats(stats, combine):
    pipes, tensors, dps = (lax.axis_size(a) for a in AXES)

    def everywhere(value, route):
        cells = [(p, t, d) for p in range(pipes) for t in range(tensors) for d in range(dps)]
        return send(value, [(c, route(*c)) for c in cells])

    for axis, size in enumerate((pipes, tensors, dps)):
        bit = 1
        while bit < size:
            flips = [bit if i == axis else 0 for i in range(3)]
            other = everywhere(stats, lambda *c, f=flips: tuple(i ^ j for i, j in zip(c, f)))
            stats = combine(stats, other)
            bit *= 2
    return stats


def combine_stats(first, second):
    top = jnp.maximum(first[0], second[0])
    total = first[1] * jnp.exp(first[0] - top) + second[1] * jnp.exp(second[0] - top)
    return jnp.stack([top, total, first[2] + second[2], first[3] + second[3]])


def local(
    inputs,
    layer_gain,
    up_weight,
    down_weight,
    final_gain,
    value_head,
    q_head,
    target_head,
    actions,
    rewards,
    done,
    order,
):
    sections = lax.axis_size("pipe")
    micro = inputs.shape[0]
    window = inputs.shape[1]
    width_model = inputs.shape[2]
    share = width_model // lax.axis_size("dp")
    w_up, w_down = up_weight[0], down_weight[0]
    gain = lax.dynamic_slice_in_dim(layer_gain[0], lax.axis_index("dp") * share, share, 0)

    columns_here = q_head.shape[1]
    offset = lax.axis_index(AXES) * columns_here
    action = jnp.take(actions, order, axis=0).reshape(-1)
    reward = jnp.take(rewards, order, axis=0).reshape(-1).astype(jnp.float32)
    finished = jnp.take(done, order, axis=0).reshape(-1).astype(jnp.float32)
    hit = action[:, None] == offset + lax.broadcasted_iota(jnp.int32, (1, columns_here), 1)
    target_rows = lax.dot_general(
        hit.astype(jnp.bfloat16),
        target_head,
        (((1,), (1,)), ((), ())),
        preferred_element_type=jnp.float32,
    ).astype(jnp.bfloat16)
    target_rows = lax.optimization_barrier(target_rows)

    chosen = jnp.take(inputs, order, axis=0)
    streams = [first_states(chosen[m]) for m in range(micro)]
    for pipe in range(sections):
        for m in range(micro):
            total = hidden_layer(streams[m], gain, w_up, w_down, pipe)
            if pipe < sections - 1:
                streams[m] = handed_on(streams[m], total, next_hops(pipe, sections))
            else:
                streams[m] = final_states(streams[m], total)
    raw = jnp.concatenate(streams, axis=0)

    wide = raw.astype(jnp.float32)
    scale_row = lax.rsqrt(jnp.mean(wide * wide, axis=-1, keepdims=True) + EPS)
    flat = (wide * scale_row * final_gain).astype(jnp.bfloat16)
    count = flat.shape[0]
    factor = width_model ** (-0.5)
    values = jnp.dot(flat, value_head, preferred_element_type=jnp.float32) * factor
    logits = jnp.dot(flat, q_head, preferred_element_type=jnp.float32) * factor
    local_top = jnp.max(logits, axis=-1)
    local_total = jnp.sum(jnp.exp(logits - local_top[:, None]), axis=-1)
    taken_part = jnp.sum(jnp.where(hit, logits, 0.0), axis=-1)
    target_part = (
        jnp.sum(flat.astype(jnp.float32) * target_rows.astype(jnp.float32), axis=-1) * factor
    )
    stats = merged_stats(
        jnp.stack([local_top, local_total, taken_part, target_part]), combine_stats
    )
    highest, summed, taken, target_taken = stats[0], stats[1], stats[2], stats[3]
    lse = highest + jnp.log(summed)
    windows = values.reshape(-1, window)
    following = jnp.concatenate(
        [windows[:, 1:], jnp.zeros((windows.shape[0], 1), jnp.float32)], axis=1
    ).reshape(-1)
    bootstrap = 0.5 * reward + GAMMA * (1.0 - finished) * following
    td_value = taken - bootstrap
    advantage = target_taken - values
    weight = jnp.where(advantage < 0, 1.0 - TAU, TAU)
    value_loss = jnp.mean(weight * advantage * advantage)
    q_loss = jnp.mean(td_value * td_value + ALPHA * (lse - taken))
    probs = jnp.exp(logits - lse[:, None]).astype(jnp.bfloat16)
    scale = VQ * factor / count
    gathered_sum = lax.dot_general(
        flat, probs, (((0,), (0,)), ((), ())), preferred_element_type=jnp.float32
    )
    lse_grad = (gathered_sum * scale).astype(jnp.bfloat16)
    shape = (micro, count // micro)
    return (
        values.reshape(shape),
        advantage.reshape(shape),
        td_value.reshape(shape),
        value_loss,
        q_loss,
        lse_grad,
    )


def solution(mesh):
    in_specs = (
        P(None, "dp", None),
        P("pipe", None),
        P("pipe", "dp", "tensor"),
        P("pipe", "tensor", "dp"),
        P(),
        P(),
        P(None, ("pipe", "tensor", "dp")),
        P(None, ("pipe", "tensor", "dp")),
        P(),
        P(),
        P(),
        P(),
    )
    out_specs = (P(), P(), P(), P(), P(), P(None, ("pipe", "tensor", "dp")))
    return jax.shard_map(local, mesh=mesh, in_specs=in_specs, out_specs=out_specs, check_vma=False)
```

time: 2730 us -> 842 us (0.31)
  waiting for transfers between devices: 2180 us -> 167 us
  starting transfers between devices: 8.4 us -> 457 us
  blocking collectives: 207 us -> 0 us
  matrix products: 248 us -> 154 us
  local copies, waits for them, and re-layouts: 43.2 us -> 12.4 us
    all_gather x4 -> x0, waiting for transfers between devices: 2010 us -> none  [the longest x1 977 us: local(): lax.all_gather(local_weights[0], 'dp', axis=0, tiled=True)]
    ppermute x5 -> x137, starting transfers between devices: 8 us -> 457 us  [send(): return lax.ppermute(block, AXES, [(flat(a), flat(b)) for a, b in pairs])]
    all_gather x7 -> x0, blocking collectives: 167 us -> none  [the longest x2 130 us: merged(): gathered = jax.tree.map(lambda a: lax.all_gather(a, axis), part)]
    ppermute x5 -> x137, waiting for transfers between devices: 5.62 us -> 167 us  [send(): return lax.ppermute(block, AXES, [(flat(a), flat(b)) for a, b in pairs])]
    reduce_scatter x5 -> x0, waiting for transfers between devices: 121 us -> none  [forward(): lax.psum_scatter(jnp.dot(hidden, w_down, preferred_element_type=jnp.float...]
    dot_general x10 -> x65, matrix products: 218 us -> 123 us  [the longest x32 59.8 us: part(): return jnp.dot(scaled, columns, preferred_element_type=jnp.float32)]
    psum x1 -> x0, waiting for transfers between devices: 41.2 us -> none  [spread(): return lax.psum(kept, axis)]
    psum x1 -> x0, blocking collectives: 40.1 us -> none  [local(): lax.psum((taken_part, target_part), ('pipe', 'tensor', 'dp'))]
  transfers between devices with their start and end apart: 15 -> 137, of which waited for: 15 -> 30; matrix products, arithmetic and copies ran while one was open for 2% -> 19% of each run, Pallas kernels for 0% -> 0%
where the time goes in v1:
time: 842 us; the launch traced here: 831 us
  starting transfers between devices  457 us (54%)
  waiting for transfers between devices  167 us (20%)
  matrix products  154 us (18%)
  other arithmetic  32.9 us (4%)
  local copies, waits for them, and re-layouts  12.4 us (1%)
    ppermute x137, starting transfers between devices, send(): return lax.ppermute(block, AXES, [(flat(a), flat(b)) for a, b in pairs])  457 us
    ppermute x137, waiting for transfers between devices, send(): return lax.ppermute(block, AXES, [(flat(a), flat(b)) for a, b in pairs])  167 us
    dot_general x32, matrix products, part(): return jnp.dot(scaled, columns, preferred_element_type=jnp.float32)  59.8 us
    dot_general x32, matrix products, hidden_layer(): total = total + jnp.dot(piece, weights, preferred_element_type=jnp.float32)  49.4 us
  transfers between devices with their start and end apart: 137, of which 30 were waited for; matrix products, arithmetic and copies ran while one was open for 19% of the time, Pallas kernels for 0%

profile of v1, /device:TPU:0, one launch (start us, length us, event | category | flops | bytes accessed | tf_op | source)
XLA Modules:
  0.0 830.9 jit_solution(2105760998742840931)
XLA Ops:
  3.1 8.4 %collective-permute-start.2 = (bf16[64,1024]{1,0:T(8,128)(2,1)S(1)}, bf16[64,1024]{1,0:T(8,128)(2,1)S(1)}, u32[]{:S(2)}, u32[]{:S(2)}) collective-permute-start(bf16[64,1024]{1,0:T(8,128)(2,1)S(1)} %get-tuple-element.40), channel_id=1, source_target_pairs={{0,3},{3,0},{1,2},{2,1},{4,7},{7,4},{5,6},{6,5},{16,19},{19,16},{1... | collective-permute-start | bytes 393224 | tf_op jit(solution)/shard_map/ppermute | solution.py:23
  11.5 4.7 collective-permute-start.1
  16.2 3.4 collective-permute-start
  19.8 3.8 collective-permute-start.68
  23.6 4.7 collective-permute-start.67
  29.1 3.4 collective-permute-start.66
  33.7 4.6 fusion.493
  38.3 3.3 collective-permute-start.3
  43.0 4.7 fusion.489
  51.6 4.5 add_convert_fusion.23
  56.2 5.4 collective-permute-start.6
  63.7 4.2 collective-permute-start.8
  71.9 3.8 add_convert_fusion.11
  75.7 3.7 collective-permute-start.72
  85.1 4.3 collective-permute-start.9
  93.7 6.3 collective-permute-start.5
  102.1 8.6 %collective-permute-start.71 = (bf16[256,1792]{1,0:T(8,128)(2,1)S(1)}, bf16[256,1792]{1,0:T(8,128)(2,1)S(1)}, u32[]{:S(2)}, u32[]{:S(2)}) collective-permute-start(bf16[256,1792]{1,0:T(8,128)(2,1)S(1)} %add_convert_fusion.10), channel_id=1, source_target_pairs={{0,1},{1,0},{2,3},{3,2},{4,5},{5,4},{6,7},{7,6},{16,17},{17,16},{1... | collective-permute-start | bytes 2752520 | tf_op jit(solution)/shard_map/ppermute | solution.py:23
  114.0 7.3 collective-permute-start.10
  123.7 4.2 collective-permute-start.76
  129.5 3.4 collective-permute-done.10
  136.1 6.7 collective-permute-done.76
  143.5 3.4 fusion.67
  147.0 3.6 fusion.59
  153.5 3.4 fusion.51
  156.9 3.4 fusion.43
  163.1 14.7 %collective-permute-done.14 = bf16[256,1792]{1,0:T(8,128)(2,1)S(1)} collective-permute-done((bf16[256,1792]{1,0:T(8,128)(2,1)}, bf16[256,1792]{1,0:T(8,128)(2,1)S(1)}, u32[]{:S(2)}, u32[]{:S(2)}) %collective-permute-start.14) | collective-permute-done | bytes 917536 | tf_op jit(solution)/shard_map/ppermute | solution.py:23
  183.4 4.2 collective-permute-done.80
  214.4 3.2 add_convert_fusion.7
  247.7 17.8 %collective-permute-done.31 = bf16[256,1792]{1,0:T(8,128)(2,1)S(1)} collective-permute-done((bf16[256,1792]{1,0:T(8,128)(2,1)S(1)}, bf16[256,1792]{1,0:T(8,128)(2,1)S(1)}, u32[]{:S(2)}, u32[]{:S(2)}) %collective-permute-start.31) | collective-permute-done | bytes 917536 | tf_op jit(solution)/shard_map/ppermute | solution.py:23
  266.7 4.4 collective-permute-start.34
  273.1 3.9 collective-permute-start.102
  278.9 6.3 collective-permute-done.97
  286.4 4.6 collective-permute-start.100
  292.2 12.7 %collective-permute-done.36 = f32[256]{0:T(256)S(1)} collective-permute-done((f32[256]{0:T(256)S(1)}, f32[256]{0:T(256)S(1)}, u32[]{:S(2)}, u32[]{:S(2)}) %collective-permute-start.36) | collective-permute-done | bytes 1056 | tf_op jit(solution)/shard_map/ppermute | solution.py:23
  304.9 4.8 collective-permute-start.37
  318.5 4.9 collective-permute-start.33
  324.3 3.2 add_convert_fusion.4
  327.5 19.9 %collective-permute-start.99 = (bf16[256,1792]{1,0:T(8,128)(2,1)}, bf16[256,1792]{1,0:T(8,128)(2,1)S(1)}, u32[]{:S(2)}, u32[]{:S(2)}) collective-permute-start(bf16[256,1792]{1,0:T(8,128)(2,1)} %add_convert_fusion.4), channel_id=1, source_target_pairs={{0,1},{1,0},{2,3},{3,2},{4,5},{5,4},{6,7},{7,6},{16,17},{17,16},{1... | collective-permute-start | bytes 2752520 | tf_op jit(solution)/shard_map/ppermute | solution.py:23
  348.9 5.7 collective-permute-start.38
  354.6 14.2 %collective-permute-done.99 = bf16[256,1792]{1,0:T(8,128)(2,1)S(1)} collective-permute-done((bf16[256,1792]{1,0:T(8,128)(2,1)}, bf16[256,1792]{1,0:T(8,128)(2,1)S(1)}, u32[]{:S(2)}, u32[]{:S(2)}) %collective-permute-start.99) | collective-permute-done | bytes 917536 | tf_op jit(solution)/shard_map/ppermute | solution.py:23
  372.2 9.0 %collective-permute-done.38 = bf16[256,1792]{1,0:T(8,128)(2,1)S(1)} collective-permute-done((bf16[256,1792]{1,0:T(8,128)(2,1)S(1)}, bf16[256,1792]{1,0:T(8,128)(2,1)S(1)}, u32[]{:S(2)}, u32[]{:S(2)}) %collective-permute-start.38) | collective-permute-done | bytes 917536 | tf_op jit(solution)/shard_map/ppermute | solution.py:23
  383.2 7.8 collective-permute-done.104
  402.0 18.6 %collective-permute-done.42 = bf16[256,1792]{1,0:T(8,128)(2,1)} collective-permute-done((bf16[256,1792]{1,0:T(8,128)(2,1)S(1)}, bf16[256,1792]{1,0:T(8,128)(2,1)}, u32[]{:S(2)}, u32[]{:S(2)}) %collective-permute-start.42) | collective-permute-done | bytes 917536 | tf_op jit(solution)/shard_map/ppermute | solution.py:23
  423.0 7.1 collective-permute-start.44
  438.9 3.4 collective-permute-done.110
  480.0 165.3 %collective-permute-start.58 = (bf16[256,1024]{1,0:T(8,128)(2,1)S(1)}, bf16[256,1024]{1,0:T(8,128)(2,1)S(1)}, u32[]{:S(2)}, u32[]{:S(2)}) collective-permute-start(bf16[256,1024]{1,0:T(8,128)(2,1)S(1)} %fusion.220), channel_id=1, source_target_pairs={{24,20},{25,21},{26,22},{27,23},{28,16},{29,17},{30,18},{31,19}} | collective-permute-start | bytes 1572872 | tf_op jit(solution)/shard_map/ppermute | solution.py:23
  645.2 7.0 collective-permute-start.57
  653.5 6.8 collective-permute-start.124
  660.2 6.8 collective-permute-start.123
  670.1 8.4 %collective-permute-done.59 = bf16[256,1024]{1,0:T(8,128)(2,1)} collective-permute-done((bf16[256,1024]{1,0:T(8,128)(2,1)S(1)}, bf16[256,1024]{1,0:T(8,128)(2,1)}, u32[]{:S(2)}, u32[]{:S(2)}) %collective-permute-start.59) | collective-permute-done | bytes 524320 | tf_op jit(solution)/shard_map/ppermute | solution.py:23
  680.8 3.8 collective-permute-start.60
  690.0 5.3 collective-permute-start.126
  710.7 5.4 collective-permute-done.129
  717.2 4.6 collective-permute-done.64
  731.1 13.8 %convolution_convert_fusion = bf16[512,4096]{1,0:T(8,128)(2,1)} fusion(bf16[4096,2048]{1,0:T(8,128)(2,1)} %param.21, s32[2048]{0:T(1024)S(1)} %iota_add_fusion, s32[512]{0:T(512)S(1)} %bitcast.388), kind=kOutput, calls=%fused_computation.11 | convolution fusion | flops 8593080320 | bytes 20981760 | tf_op jit(solution)/shard_map/dot_general | solution.py:202
  753.5 12.7 %fusion.497 = (f32[512]{0:T(512)S(1)}, f32[512,2048]{1,0:T(8,128)S(1)}) fusion(bf16[4096,2048]{1,0:T(8,128)(2,1)} %param.20, f32[4096]{0:T(1024)S(1)} %copy-done.17, f32[512]{0:T(512)S(1)} %add_rsqrt_fusion, bf16[256,4096]{1,0:T(8,128)(2,1)S(1)} %broadcast_select_fusion, bf16[256,4096]{1,0:T(8,128)(2,1)S(1)} %broadcast_select_fusion.1), kind=kOutput, calls=%fused_computation.534 | convolution fusion | flops 8606711808 | bytes 25186304 | tf_op jit(solution)/shard_map/dot_general | solution.py:227
  769.3 3.2 collective-permute-start.132
  773.6 5.6 collective-permute-start.133
  779.2 3.5 collective-permute-done.133
  782.8 4.5 collective-permute-start.134
  787.3 3.5 collective-permute-done.134
  790.8 4.5 collective-permute-start.135
  798.9 4.7 collective-permute-start.136
  812.7 15.5 %multiply_convert_fusion = bf16[4096,2048]{1,0:T(8,128)(2,1)} fusion(f32[512,2048]{1,0:T(8,128)} %copy-done.8, f32[512]{0:T(512)S(1)} %get-tuple-element.10, f32[4096]{0:T(1024)S(1)} %copy-done.17, f32[512]{0:T(512)S(1)} %add_rsqrt_fusion, bf16[256,4096]{1,0:T(8,128)(2,1)} %copy-done.2, bf16[256,4096]{1,0:T(8,128)(2,1)S(1)} %broadcast_select_fusion.1), kind=kOutput, calls=%fused_computation.4 | convolution fusion | flops 8623489024 | bytes 25186304 | tf_op jit(solution)/shard_map/dot_general | solution.py:251
  (462 shorter events, 250.7 us)
Async XLA Ops:
  3.1 29.4 %collective-permute-start.2 = (bf16[64,1024]{1,0:T(8,128)(2,1)S(1)}, bf16[64,1024]{1,0:T(8,128)(2,1)S(1)}, u32[]{:S(2)}, u32[]{:S(2)}) collective-permute-start(bf16[64,1024]{1,0:T(8,128)(2,1)S(1)} %get-tuple-element.40), channel_id=1, source_target_pairs={{0,3},{3,0},{1,2},{2,1},{4,7},{7,4},{5,6},{6,5},{16,19},{19,16},{1... | collective-permute-start | bytes 393224 | tf_op jit(solution)/shard_map/ppermute | solution.py:23
  11.5 21.0 %collective-permute-start.1 = (bf16[64,1024]{1,0:T(8,128)(2,1)S(1)}, bf16[64,1024]{1,0:T(8,128)(2,1)S(1)}, u32[]{:S(2)}, u32[]{:S(2)}) collective-permute-start(bf16[64,1024]{1,0:T(8,128)(2,1)S(1)} %get-tuple-element.41), channel_id=1, source_target_pairs={{0,2},{2,0},{1,3},{3,1},{4,6},{6,4},{5,7},{7,5},{16,18},{18,16},{1... | collective-permute-start | bytes 393224 | tf_op jit(solution)/shard_map/ppermute | solution.py:23
  16.2 12.8 %collective-permute-start = (bf16[64,1024]{1,0:T(8,128)(2,1)S(1)}, bf16[64,1024]{1,0:T(8,128)(2,1)S(1)}, u32[]{:S(2)}, u32[]{:S(2)}) collective-permute-start(bf16[64,1024]{1,0:T(8,128)(2,1)S(1)} %get-tuple-element.42), channel_id=1, source_target_pairs={{0,1},{1,0},{2,3},{3,2},{4,5},{5,4},{6,7},{7,6},{16,17},{17,16},{1... | collective-permute-start | bytes 393224 | tf_op jit(solution)/shard_map/ppermute | solution.py:23
  19.8 22.0 %collective-permute-start.68 = (bf16[64,1024]{1,0:T(8,128)(2,1)S(1)}, bf16[64,1024]{1,0:T(8,128)(2,1)S(1)}, u32[]{:S(2)}, u32[]{:S(2)}) collective-permute-start(bf16[64,1024]{1,0:T(8,128)(2,1)S(1)} %get-tuple-element.47), channel_id=1, source_target_pairs={{0,3},{3,0},{1,2},{2,1},{4,7},{7,4},{5,6},{6,5},{16,19},{19,16},{1... | collective-permute-start | bytes 393224 | tf_op jit(solution)/shard_map/ppermute | solution.py:23
  23.6 18.1 %collective-permute-start.67 = (bf16[64,1024]{1,0:T(8,128)(2,1)S(1)}, bf16[64,1024]{1,0:T(8,128)(2,1)S(1)}, u32[]{:S(2)}, u32[]{:S(2)}) collective-permute-start(bf16[64,1024]{1,0:T(8,128)(2,1)S(1)} %get-tuple-element.48), channel_id=1, source_target_pairs={{0,2},{2,0},{1,3},{3,1},{4,6},{6,4},{5,7},{7,5},{16,18},{18,16},{1... | collective-permute-start | bytes 393224 | tf_op jit(solution)/shard_map/ppermute | solution.py:23
  38.3 13.3 %collective-permute-start.3 = (bf16[256,1792]{1,0:T(8,128)(2,1)S(1)}, bf16[256,1792]{1,0:T(8,128)(2,1)}, u32[]{:S(2)}, u32[]{:S(2)}) collective-permute-start(bf16[256,1792]{1,0:T(8,128)(2,1)S(1)} %get-tuple-element.104), channel_id=1, source_target_pairs={{0,1},{3,2},{4,5},{7,6},{16,17},{19,18},{20,21},{23,22}} | collective-permute-start | bytes 2752520 | tf_op jit(solution)/shard_map/ppermute | solution.py:23
  47.7 24.2 %collective-permute-start.69 = (bf16[256,1792]{1,0:T(8,128)(2,1)}, bf16[256,1792]{1,0:T(8,128)(2,1)}, u32[]{:S(2)}, u32[]{:S(2)}) collective-permute-start(bf16[256,1792]{1,0:T(8,128)(2,1)} %get-tuple-element.96), channel_id=1, source_target_pairs={{0,1},{3,2},{4,5},{7,6},{16,17},{19,18},{20,21},{23,22}} | collective-permute-start | bytes 2752520 | tf_op jit(solution)/shard_map/ppermute | solution.py:23
  56.2 33.3 %collective-permute-start.6 = (bf16[256,1792]{1,0:T(8,128)(2,1)}, bf16[256,1792]{1,0:T(8,128)(2,1)}, u32[]{:S(2)}, u32[]{:S(2)}) collective-permute-start(bf16[256,1792]{1,0:T(8,128)(2,1)} %add_convert_fusion.23), channel_id=1, source_target_pairs={{0,1},{3,2},{4,5},{7,6},{16,17},{19,18},{20,21},{23,22}} | collective-permute-start | bytes 2752520 | tf_op jit(solution)/shard_map/ppermute | solution.py:23
  61.7 20.9 %collective-permute-start.74 = (f32[256]{0:T(256)S(1)}, f32[256]{0:T(256)S(1)}, u32[]{:S(2)}, u32[]{:S(2)}) collective-permute-start(f32[256]{0:T(256)S(1)} %reduce_sum.138), channel_id=1, source_target_pairs={{0,1},{1,0},{2,3},{3,2},{4,5},{5,4},{6,7},{7,6},{16,17},{17,16},{1... | collective-permute-start | bytes 3080 | tf_op jit(solution)/shard_map/ppermute | solution.py:23
  63.7 21.4 %collective-permute-start.8 = (f32[256]{0:T(256)S(1)}, f32[256]{0:T(256)S(1)}, u32[]{:S(2)}, u32[]{:S(2)}) collective-permute-start(f32[256]{0:T(256)S(1)} %reduce_sum.133), channel_id=1, source_target_pairs={{0,1},{1,0},{2,3},{3,2},{4,5},{5,4},{6,7},{7,6},{16,17},{17,16},{1... | collective-permute-start | bytes 3080 | tf_op jit(solution)/shard_map/ppermute | solution.py:23
  71.0 20.5 %collective-permute-start.4 = (bf16[256,1792]{1,0:T(8,128)(2,1)}, bf16[256,1792]{1,0:T(8,128)(2,1)S(1)}, u32[]{:S(2)}, u32[]{:S(2)}) collective-permute-start(bf16[256,1792]{1,0:T(8,128)(2,1)} %add_convert_fusion.23), channel_id=1, source_target_pairs={{1,2},{2,1},{5,6},{6,5},{17,18},{18,17},{21,22},{22,21}} | collective-permute-start | bytes 2752520 | tf_op jit(solution)/shard_map/ppermute | solution.py:23
  75.7 18.0 %collective-permute-start.72 = (bf16[256,1792]{1,0:T(8,128)(2,1)S(1)}, bf16[256,1792]{1,0:T(8,128)(2,1)S(1)}, u32[]{:S(2)}, u32[]{:S(2)}) collective-permute-start(bf16[256,1792]{1,0:T(8,128)(2,1)S(1)} %add_convert_fusion.11), channel_id=1, source_target_pairs={{0,1},{3,2},{4,5},{7,6},{16,17},{19,18},{20,21},{23,22}} | collective-permute-start | bytes 2752520 | tf_op jit(solution)/shard_map/ppermute | solution.py:23
  82.6 19.5 %collective-permute-start.75 = (f32[256]{0:T(256)S(1)}, f32[256]{0:T(256)S(1)}, u32[]{:S(2)}, u32[]{:S(2)}) collective-permute-start(f32[256]{0:T(256)S(1)} %add.717), channel_id=1, source_target_pairs={{0,2},{2,0},{1,3},{3,1},{4,6},{6,4},{5,7},{7,5},{16,18},{18,16},{1... | collective-permute-start | bytes 3080 | tf_op jit(solution)/shard_map/ppermute | solution.py:23
  85.1 25.7 %collective-permute-start.9 = (f32[256]{0:T(256)S(1)}, f32[256]{0:T(256)S(1)}, u32[]{:S(2)}, u32[]{:S(2)}) collective-permute-start(f32[256]{0:T(256)S(1)} %add.661), channel_id=1, source_target_pairs={{0,2},{2,0},{1,3},{3,1},{4,6},{6,4},{5,7},{7,5},{16,18},{18,16},{1... | collective-permute-start | bytes 3080 | tf_op jit(solution)/shard_map/ppermute | solution.py:23
  91.6 19.2 %collective-permute-start.7 = (bf16[256,1792]{1,0:T(8,128)(2,1)S(1)}, bf16[256,1792]{1,0:T(8,128)(2,1)S(1)}, u32[]{:S(2)}, u32[]{:S(2)}) collective-permute-start(bf16[256,1792]{1,0:T(8,128)(2,1)S(1)} %add_convert_fusion.21), channel_id=1, source_target_pairs={{1,2},{2,1},{5,6},{6,5},{17,18},{18,17},{21,22},{22,21}} | collective-permute-start | bytes 2752520 | tf_op jit(solution)/shard_map/ppermute | solution.py:23
  93.7 17.7 %collective-permute-start.5 = (bf16[256,1792]{1,0:T(8,128)(2,1)S(1)}, bf16[256,1792]{1,0:T(8,128)(2,1)S(1)}, u32[]{:S(2)}, u32[]{:S(2)}) collective-permute-start(bf16[256,1792]{1,0:T(8,128)(2,1)S(1)} %add_convert_fusion.22), channel_id=1, source_target_pairs={{0,1},{1,0},{2,3},{3,2},{4,5},{5,4},{6,7},{7,6},{16,17},{17,16},{1... | collective-permute-start | bytes 2752520 | tf_op jit(solution)/shard_map/ppermute | solution.py:23
  100.2 21.1 %collective-permute-start.73 = (bf16[256,1792]{1,0:T(8,128)(2,1)S(1)}, bf16[256,1792]{1,0:T(8,128)(2,1)S(1)}, u32[]{:S(2)}, u32[]{:S(2)}) collective-permute-start(bf16[256,1792]{1,0:T(8,128)(2,1)S(1)} %add_convert_fusion.9), channel_id=1, source_target_pairs={{1,2},{2,1},{5,6},{6,5},{17,18},{18,17},{21,22},{22,21}} | collective-permute-start | bytes 2752520 | tf_op jit(solution)/shard_map/ppermute | solution.py:23
  102.1 20.0 %collective-permute-start.71 = (bf16[256,1792]{1,0:T(8,128)(2,1)S(1)}, bf16[256,1792]{1,0:T(8,128)(2,1)S(1)}, u32[]{:S(2)}, u32[]{:S(2)}) collective-permute-start(bf16[256,1792]{1,0:T(8,128)(2,1)S(1)} %add_convert_fusion.10), channel_id=1, source_target_pairs={{0,1},{1,0},{2,3},{3,2},{4,5},{5,4},{6,7},{7,6},{16,17},{17,16},{1... | collective-permute-start | bytes 2752520 | tf_op jit(solution)/shard_map/ppermute | solution.py:23
  113.0 21.5 %collective-permute-start.12 = (bf16[256,1792]{1,0:T(8,128)(2,1)}, bf16[256,1792]{1,0:T(8,128)(2,1)S(1)}, u32[]{:S(2)}, u32[]{:S(2)}) collective-permute-start(bf16[256,1792]{1,0:T(8,128)(2,1)} %multiply_convert_fusion.8), channel_id=1, source_target_pairs={{1,2},{2,1},{5,6},{6,5},{17,18},{18,17},{21,22},{22,21}} | collective-permute-start | bytes 2752520 | tf_op jit(solution)/shard_map/ppermute | solution.py:23
  114.0 19.0 %collective-permute-start.10 = (bf16[256,1792]{1,0:T(8,128)(2,1)}, bf16[256,1792]{1,0:T(8,128)(2,1)}, u32[]{:S(2)}, u32[]{:S(2)}) collective-permute-start(bf16[256,1792]{1,0:T(8,128)(2,1)} %multiply_convert_fusion.8), channel_id=1, source_target_pairs={{0,1},{1,0},{2,3},{3,2},{4,5},{5,4},{6,7},{7,6},{16,17},{17,16},{1... | collective-permute-start | bytes 2752520 | tf_op jit(solution)/shard_map/ppermute | solution.py:23
  123.7 19.0 %collective-permute-start.76 = (bf16[256,1792]{1,0:T(8,128)(2,1)}, bf16[256,1792]{1,0:T(8,128)(2,1)}, u32[]{:S(2)}, u32[]{:S(2)}) collective-permute-start(bf16[256,1792]{1,0:T(8,128)(2,1)} %multiply_convert_fusion.4), channel_id=1, source_target_pairs={{0,1},{1,0},{2,3},{3,2},{4,5},{5,4},{6,7},{7,6},{16,17},{17,16},{1... | collective-permute-start | bytes 2752520 | tf_op jit(solution)/shard_map/ppermute | solution.py:23
  127.9 22.6 %collective-permute-start.78 = (bf16[256,1792]{1,0:T(8,128)(2,1)}, bf16[256,1792]{1,0:T(8,128)(2,1)}, u32[]{:S(2)}, u32[]{:S(2)}) collective-permute-start(bf16[256,1792]{1,0:T(8,128)(2,1)} %multiply_convert_fusion.4), channel_id=1, source_target_pairs={{1,2},{2,1},{5,6},{6,5},{17,18},{18,17},{21,22},{22,21}} | collective-permute-start | bytes 2752520 | tf_op jit(solution)/shard_map/ppermute | solution.py:23
  133.0 19.2 %collective-permute-start.11 = (bf16[256,1792]{1,0:T(8,128)(2,1)}, bf16[256,1792]{1,0:T(8,128)(2,1)}, u32[]{:S(2)}, u32[]{:S(2)}) collective-permute-start(bf16[256,1792]{1,0:T(8,128)(2,1)} %collective-permute-done.10), channel_id=1, source_target_pairs={{1,2},{2,1},{5,6},{6,5},{17,18},{18,17},{21,22},{22,21}} | collective-permute-start | bytes 2752520 | tf_op jit(solution)/shard_map/ppermute | solution.py:23
  134.6 27.3 %collective-permute-start.13 = (bf16[256,1792]{1,0:T(8,128)(2,1)S(1)}, bf16[256,1792]{1,0:T(8,128)(2,1)S(1)}, u32[]{:S(2)}, u32[]{:S(2)}) collective-permute-start(bf16[256,1792]{1,0:T(8,128)(2,1)S(1)} %collective-permute-done.12), channel_id=1, source_target_pairs={{1,0},{2,3},{5,4},{6,7},{17,16},{18,19},{21,20},{22,23}} | collective-permute-start | bytes 2752520 | tf_op jit(solution)/shard_map/ppermute | solution.py:23
  142.8 17.6 %collective-permute-start.77 = (bf16[256,1792]{1,0:T(8,128)(2,1)}, bf16[256,1792]{1,0:T(8,128)(2,1)S(1)}, u32[]{:S(2)}, u32[]{:S(2)}) collective-permute-start(bf16[256,1792]{1,0:T(8,128)(2,1)} %collective-permute-done.76), channel_id=1, source_target_pairs={{1,2},{2,1},{5,6},{6,5},{17,18},{18,17},{21,22},{22,21}} | collective-permute-start | bytes 2752520 | tf_op jit(solution)/shard_map/ppermute | solution.py:23
  150.6 31.6 %collective-permute-start.79 = (bf16[256,1792]{1,0:T(8,128)(2,1)}, bf16[256,1792]{1,0:T(8,128)(2,1)S(1)}, u32[]{:S(2)}, u32[]{:S(2)}) collective-permute-start(bf16[256,1792]{1,0:T(8,128)(2,1)} %collective-permute-done.78), channel_id=1, source_target_pairs={{1,0},{2,3},{5,4},{6,7},{17,16},{18,19},{21,20},{22,23}} | collective-permute-start | bytes 2752520 | tf_op jit(solution)/shard_map/ppermute | solution.py:23
  152.2 25.6 %collective-permute-start.14 = (bf16[256,1792]{1,0:T(8,128)(2,1)}, bf16[256,1792]{1,0:T(8,128)(2,1)S(1)}, u32[]{:S(2)}, u32[]{:S(2)}) collective-permute-start(bf16[256,1792]{1,0:T(8,128)(2,1)} %collective-permute-done.11), channel_id=1, source_target_pairs={{1,0},{2,3},{5,4},{6,7},{17,16},{18,19},{21,20},{22,23}} | collective-permute-start | bytes 2752520 | tf_op jit(solution)/shard_map/ppermute | solution.py:23
  160.4 27.2 %collective-permute-start.80 = (bf16[256,1792]{1,0:T(8,128)(2,1)S(1)}, bf16[256,1792]{1,0:T(8,128)(2,1)S(1)}, u32[]{:S(2)}, u32[]{:S(2)}) collective-permute-start(bf16[256,1792]{1,0:T(8,128)(2,1)S(1)} %collective-permute-done.77), channel_id=1, source_target_pairs={{1,0},{2,3},{5,4},{6,7},{17,16},{18,19},{21,20},{22,23}} | collective-permute-start | bytes 2752520 | tf_op jit(solution)/shard_map/ppermute | solution.py:23
  243.2 22.3 %collective-permute-start.31 = (bf16[256,1792]{1,0:T(8,128)(2,1)S(1)}, bf16[256,1792]{1,0:T(8,128)(2,1)S(1)}, u32[]{:S(2)}, u32[]{:S(2)}) collective-permute-start(bf16[256,1792]{1,0:T(8,128)(2,1)S(1)} %get-tuple-element.108), channel_id=1, source_target_pairs={{0,1},{3,2},{4,5},{7,6},{16,17},{19,18},{20,21},{23,22}} | collective-permute-start | bytes 2752520 | tf_op jit(solution)/shard_map/ppermute | solution.py:23
  246.3 38.8 %collective-permute-start.97 = (bf16[256,1792]{1,0:T(8,128)(2,1)S(1)}, bf16[256,1792]{1,0:T(8,128)(2,1)S(1)}, u32[]{:S(2)}, u32[]{:S(2)}) collective-permute-start(bf16[256,1792]{1,0:T(8,128)(2,1)S(1)} %get-tuple-element.100), channel_id=1, source_target_pairs={{0,1},{3,2},{4,5},{7,6},{16,17},{19,18},{20,21},{23,22}} | collective-permute-start | bytes 2752520 | tf_op jit(solution)/shard_map/ppermute | solution.py:23
  266.7 44.9 %collective-permute-start.34 = (bf16[256,1792]{1,0:T(8,128)(2,1)S(1)}, bf16[256,1792]{1,0:T(8,128)(2,1)S(1)}, u32[]{:S(2)}, u32[]{:S(2)}) collective-permute-start(bf16[256,1792]{1,0:T(8,128)(2,1)S(1)} %add_convert_fusion.17), channel_id=1, source_target_pairs={{0,1},{3,2},{4,5},{7,6},{16,17},{19,18},{20,21},{23,22}} | collective-permute-start | bytes 2752520 | tf_op jit(solution)/shard_map/ppermute | solution.py:23
  271.1 33.7 %collective-permute-start.36 = (f32[256]{0:T(256)S(1)}, f32[256]{0:T(256)S(1)}, u32[]{:S(2)}, u32[]{:S(2)}) collective-permute-start(f32[256]{0:T(256)S(1)} %get-tuple-element.23), channel_id=1, source_target_pairs={{0,1},{1,0},{2,3},{3,2},{4,5},{5,4},{6,7},{7,6},{16,17},{17,16},{1... | collective-permute-start | bytes 3080 | tf_op jit(solution)/shard_map/ppermute | solution.py:23
  273.1 36.6 %collective-permute-start.102 = (f32[256]{0:T(256)S(1)}, f32[256]{0:T(256)S(1)}, u32[]{:S(2)}, u32[]{:S(2)}) collective-permute-start(f32[256]{0:T(256)S(1)} %get-tuple-element.31), channel_id=1, source_target_pairs={{0,1},{1,0},{2,3},{3,2},{4,5},{5,4},{6,7},{7,6},{16,17},{17,16},{1... | collective-permute-start | bytes 3080 | tf_op jit(solution)/shard_map/ppermute | solution.py:23
  278.2 35.3 %collective-permute-start.32 = (bf16[256,1792]{1,0:T(8,128)(2,1)S(1)}, bf16[256,1792]{1,0:T(8,128)(2,1)S(1)}, u32[]{:S(2)}, u32[]{:S(2)}) collective-permute-start(bf16[256,1792]{1,0:T(8,128)(2,1)S(1)} %add_convert_fusion.17), channel_id=1, source_target_pairs={{1,2},{2,1},{5,6},{6,5},{17,18},{18,17},{21,22},{22,21}} | collective-permute-start | bytes 2752520 | tf_op jit(solution)/shard_map/ppermute | solution.py:23
  286.4 32.1 %collective-permute-start.100 = (bf16[256,1792]{1,0:T(8,128)(2,1)S(1)}, bf16[256,1792]{1,0:T(8,128)(2,1)S(1)}, u32[]{:S(2)}, u32[]{:S(2)}) collective-permute-start(bf16[256,1792]{1,0:T(8,128)(2,1)S(1)} %add_convert_fusion.5), channel_id=1, source_target_pairs={{0,1},{3,2},{4,5},{7,6},{16,17},{19,18},{20,21},{23,22}} | collective-permute-start | bytes 2752520 | tf_op jit(solution)/shard_map/ppermute | solution.py:23
  304.9 22.7 %collective-permute-start.37 = (f32[256]{0:T(256)S(1)}, f32[256]{0:T(256)S(1)}, u32[]{:S(2)}, u32[]{:S(2)}) collective-permute-start(f32[256]{0:T(256)S(1)} %add.689), channel_id=1, source_target_pairs={{0,2},{2,0},{1,3},{3,1},{4,6},{6,4},{5,7},{7,5},{16,18},{18,16},{1... | collective-permute-start | bytes 3080 | tf_op jit(solution)/shard_map/ppermute | solution.py:23
  309.7 37.8 %collective-permute-start.103 = (f32[256]{0:T(256)S(1)}, f32[256]{0:T(256)S(1)}, u32[]{:S(2)}, u32[]{:S(2)}) collective-permute-start(f32[256]{0:T(256)S(1)} %add.745), channel_id=1, source_target_pairs={{0,2},{2,0},{1,3},{3,1},{4,6},{6,4},{5,7},{7,5},{16,18},{18,16},{1... | collective-permute-start | bytes 3080 | tf_op jit(solution)/shard_map/ppermute | solution.py:23
  313.5 34.0 %collective-permute-start.35 = (bf16[256,1792]{1,0:T(8,128)(2,1)S(1)}, bf16[256,1792]{1,0:T(8,128)(2,1)S(1)}, u32[]{:S(2)}, u32[]{:S(2)}) collective-permute-start(bf16[256,1792]{1,0:T(8,128)(2,1)S(1)} %add_convert_fusion.15), channel_id=1, source_target_pairs={{1,2},{2,1},{5,6},{6,5},{17,18},{18,17},{21,22},{22,21}} | collective-permute-start | bytes 2752520 | tf_op jit(solution)/shard_map/ppermute | solution.py:23
  318.5 29.0 %collective-permute-start.33 = (bf16[256,1792]{1,0:T(8,128)(2,1)S(1)}, bf16[256,1792]{1,0:T(8,128)(2,1)S(1)}, u32[]{:S(2)}, u32[]{:S(2)}) collective-permute-start(bf16[256,1792]{1,0:T(8,128)(2,1)S(1)} %add_convert_fusion.16), channel_id=1, source_target_pairs={{0,1},{1,0},{2,3},{3,2},{4,5},{5,4},{6,7},{7,6},{16,17},{17,16},{1... | collective-permute-start | bytes 2752520 | tf_op jit(solution)/shard_map/ppermute | solution.py:23
  323.5 31.1 %collective-permute-start.101 = (bf16[256,1792]{1,0:T(8,128)(2,1)S(1)}, bf16[256,1792]{1,0:T(8,128)(2,1)S(1)}, u32[]{:S(2)}, u32[]{:S(2)}) collective-permute-start(bf16[256,1792]{1,0:T(8,128)(2,1)S(1)} %add_convert_fusion.3), channel_id=1, source_target_pairs={{1,2},{2,1},{5,6},{6,5},{17,18},{18,17},{21,22},{22,21}} | collective-permute-start | bytes 2752520 | tf_op jit(solution)/shard_map/ppermute | solution.py:23
  327.5 41.3 %collective-permute-start.99 = (bf16[256,1792]{1,0:T(8,128)(2,1)}, bf16[256,1792]{1,0:T(8,128)(2,1)S(1)}, u32[]{:S(2)}, u32[]{:S(2)}) collective-permute-start(bf16[256,1792]{1,0:T(8,128)(2,1)} %add_convert_fusion.4), channel_id=1, source_target_pairs={{0,1},{1,0},{2,3},{3,2},{4,5},{5,4},{6,7},{7,6},{16,17},{17,16},{1... | collective-permute-start | bytes 2752520 | tf_op jit(solution)/shard_map/ppermute | solution.py:23
  348.2 33.7 %collective-permute-start.40 = (bf16[256,1792]{1,0:T(8,128)(2,1)S(1)}, bf16[256,1792]{1,0:T(8,128)(2,1)S(1)}, u32[]{:S(2)}, u32[]{:S(2)}) collective-permute-start(bf16[256,1792]{1,0:T(8,128)(2,1)S(1)} %multiply_convert_fusion.6), channel_id=1, source_target_pairs={{1,2},{2,1},{5,6},{6,5},{17,18},{18,17},{21,22},{22,21}} | collective-permute-start | bytes 2752520 | tf_op jit(solution)/shard_map/ppermute | solution.py:23
  348.9 32.2 %collective-permute-start.38 = (bf16[256,1792]{1,0:T(8,128)(2,1)S(1)}, bf16[256,1792]{1,0:T(8,128)(2,1)S(1)}, u32[]{:S(2)}, u32[]{:S(2)}) collective-permute-start(bf16[256,1792]{1,0:T(8,128)(2,1)S(1)} %multiply_convert_fusion.6), channel_id=1, source_target_pairs={{0,1},{1,0},{2,3},{3,2},{4,5},{5,4},{6,7},{7,6},{16,17},{17,16},{1... | collective-permute-start | bytes 2752520 | tf_op jit(solution)/shard_map/ppermute | solution.py:23
  369.5 21.5 %collective-permute-start.104 = (bf16[256,1792]{1,0:T(8,128)(2,1)S(1)}, bf16[256,1792]{1,0:T(8,128)(2,1)S(1)}, u32[]{:S(2)}, u32[]{:S(2)}) collective-permute-start(bf16[256,1792]{1,0:T(8,128)(2,1)S(1)} %multiply_convert_fusion.2), channel_id=1, source_target_pairs={{0,1},{1,0},{2,3},{3,2},{4,5},{5,4},{6,7},{7,6},{16,17},{17,16},{1... | collective-permute-start | bytes 2752520 | tf_op jit(solution)/shard_map/ppermute | solution.py:23
  371.4 22.6 %collective-permute-start.106 = (bf16[256,1792]{1,0:T(8,128)(2,1)S(1)}, bf16[256,1792]{1,0:T(8,128)(2,1)S(1)}, u32[]{:S(2)}, u32[]{:S(2)}) collective-permute-start(bf16[256,1792]{1,0:T(8,128)(2,1)S(1)} %multiply_convert_fusion.2), channel_id=1, source_target_pairs={{1,2},{2,1},{5,6},{6,5},{17,18},{18,17},{21,22},{22,21}} | collective-permute-start | bytes 2752520 | tf_op jit(solution)/shard_map/ppermute | solution.py:23
  381.2 14.2 %collective-permute-start.39 = (bf16[256,1792]{1,0:T(8,128)(2,1)S(1)}, bf16[256,1792]{1,0:T(8,128)(2,1)S(1)}, u32[]{:S(2)}, u32[]{:S(2)}) collective-permute-start(bf16[256,1792]{1,0:T(8,128)(2,1)S(1)} %collective-permute-done.38), channel_id=1, source_target_pairs={{1,2},{2,1},{5,6},{6,5},{17,18},{18,17},{21,22},{22,21}} | collective-permute-start | bytes 2752520 | tf_op jit(solution)/shard_map/ppermute | solution.py:23
  381.9 18.9 %collective-permute-start.41 = (bf16[256,1792]{1,0:T(8,128)(2,1)S(1)}, bf16[256,1792]{1,0:T(8,128)(2,1)S(1)}, u32[]{:S(2)}, u32[]{:S(2)}) collective-permute-start(bf16[256,1792]{1,0:T(8,128)(2,1)S(1)} %collective-permute-done.40), channel_id=1, source_target_pairs={{1,0},{2,3},{5,4},{6,7},{17,16},{18,19},{21,20},{22,23}} | collective-permute-start | bytes 2752520 | tf_op jit(solution)/shard_map/ppermute | solution.py:23
  394.0 37.3 %collective-permute-start.107 = (bf16[256,1792]{1,0:T(8,128)(2,1)S(1)}, bf16[256,1792]{1,0:T(8,128)(2,1)S(1)}, u32[]{:S(2)}, u32[]{:S(2)}) collective-permute-start(bf16[256,1792]{1,0:T(8,128)(2,1)S(1)} %collective-permute-done.106), channel_id=1, source_target_pairs={{1,0},{2,3},{5,4},{6,7},{17,16},{18,19},{21,20},{22,23}} | collective-permute-start | bytes 2752520 | tf_op jit(solution)/shard_map/ppermute | solution.py:23
  395.4 25.2 %collective-permute-start.42 = (bf16[256,1792]{1,0:T(8,128)(2,1)S(1)}, bf16[256,1792]{1,0:T(8,128)(2,1)}, u32[]{:S(2)}, u32[]{:S(2)}) collective-permute-start(bf16[256,1792]{1,0:T(8,128)(2,1)S(1)} %collective-permute-done.39), channel_id=1, source_target_pairs={{1,0},{2,3},{5,4},{6,7},{17,16},{18,19},{21,20},{22,23}} | collective-permute-start | bytes 2752520 | tf_op jit(solution)/shard_map/ppermute | solution.py:23
  399.0 33.7 %collective-permute-start.108 = (bf16[256,1792]{1,0:T(8,128)(2,1)S(1)}, bf16[256,1792]{1,0:T(8,128)(2,1)S(1)}, u32[]{:S(2)}, u32[]{:S(2)}) collective-permute-start(bf16[256,1792]{1,0:T(8,128)(2,1)S(1)} %collective-permute-done.105), channel_id=1, source_target_pairs={{1,0},{2,3},{5,4},{6,7},{17,16},{18,19},{21,20},{22,23}} | collective-permute-start | bytes 2752520 | tf_op jit(solution)/shard_map/ppermute | solution.py:23
  423.0 13.7 %collective-permute-start.44 = (bf16[256,1024]{1,0:T(8,128)(2,1)S(1)}, bf16[256,1024]{1,0:T(8,128)(2,1)S(1)}, u32[]{:S(2)}, u32[]{:S(2)}) collective-permute-start(bf16[256,1024]{1,0:T(8,128)(2,1)S(1)} %fusion.223), channel_id=1, source_target_pairs={{0,12},{1,13},{2,14},{3,15},{4,8},{5,9},{6,10},{7,11},{16,28},{17,... | collective-permute-start | bytes 1572872 | tf_op jit(solution)/shard_map/ppermute | solution.py:23
  475.5 176.7 %collective-permute-start.122 = (bf16[256,1792]{1,0:T(8,128)(2,1)S(1)}, bf16[256,1792]{1,0:T(8,128)(2,1)S(1)}, u32[]{:S(2)}, u32[]{:S(2)}) collective-permute-start(bf16[256,1792]{1,0:T(8,128)(2,1)S(1)} %collective-permute-done.119), channel_id=1, source_target_pairs={{9,8},{10,11},{13,12},{14,15},{25,24},{26,27},{29,28},{30,31}} | collective-permute-start | bytes 2752520 | tf_op jit(solution)/shard_map/ppermute | solution.py:23
  480.0 187.1 %collective-permute-start.58 = (bf16[256,1024]{1,0:T(8,128)(2,1)S(1)}, bf16[256,1024]{1,0:T(8,128)(2,1)S(1)}, u32[]{:S(2)}, u32[]{:S(2)}) collective-permute-start(bf16[256,1024]{1,0:T(8,128)(2,1)S(1)} %fusion.220), channel_id=1, source_target_pairs={{24,20},{25,21},{26,22},{27,23},{28,16},{29,17},{30,18},{31,19}} | collective-permute-start | bytes 1572872 | tf_op jit(solution)/shard_map/ppermute | solution.py:23
  645.2 21.8 %collective-permute-start.57 = (bf16[256,1024]{1,0:T(8,128)(2,1)S(1)}, bf16[256,1024]{1,0:T(8,128)(2,1)S(1)}, u32[]{:S(2)}, u32[]{:S(2)}) collective-permute-start(bf16[256,1024]{1,0:T(8,128)(2,1)S(1)} %fusion.220), channel_id=1, source_target_pairs={{24,16},{25,17},{26,18},{27,19},{28,20},{29,21},{30,22},{31,23}} | collective-permute-start | bytes 1572872 | tf_op jit(solution)/shard_map/ppermute | solution.py:23
  653.5 15.1 %collective-permute-start.124 = (bf16[256,1024]{1,0:T(8,128)(2,1)S(1)}, bf16[256,1024]{1,0:T(8,128)(2,1)S(1)}, u32[]{:S(2)}, u32[]{:S(2)}) collective-permute-start(bf16[256,1024]{1,0:T(8,128)(2,1)S(1)} %fusion.208), channel_id=1, source_target_pairs={{24,20},{25,21},{26,22},{27,23},{28,16},{29,17},{30,18},{31,19}} | collective-permute-start | bytes 1572872 | tf_op jit(solution)/shard_map/ppermute | solution.py:23
  668.8 17.3 %collective-permute-start.125 = (bf16[256,1024]{1,0:T(8,128)(2,1)S(1)}, bf16[256,1024]{1,0:T(8,128)(2,1)}, u32[]{:S(2)}, u32[]{:S(2)}) collective-permute-start(bf16[256,1024]{1,0:T(8,128)(2,1)S(1)} %add_convert_fusion.24), channel_id=1, source_target_pairs={{16,0},{17,1},{18,2},{19,3},{20,4},{21,5},{22,6},{23,7}} | collective-permute-start | bytes 1572872 | tf_op jit(solution)/shard_map/ppermute | solution.py:23
  680.8 16.7 %collective-permute-start.60 = (bf16[256,1024]{1,0:T(8,128)(2,1)}, bf16[256,1024]{1,0:T(8,128)(2,1)S(1)}, u32[]{:S(2)}, u32[]{:S(2)}) collective-permute-start(bf16[256,1024]{1,0:T(8,128)(2,1)} %get-tuple-element.20), channel_id=1, source_target_pairs={{0,1},{1,0},{2,3},{3,2},{4,5},{5,4},{6,7},{7,6},{16,17},{17,16},{1... | collective-permute-start | bytes 1572872 | tf_op jit(solution)/shard_map/ppermute | solution.py:23
  684.6 13.6 %collective-permute-start.62 = (bf16[256,1024]{1,0:T(8,128)(2,1)}, bf16[256,1024]{1,0:T(8,128)(2,1)}, u32[]{:S(2)}, u32[]{:S(2)}) collective-permute-start(bf16[256,1024]{1,0:T(8,128)(2,1)} %get-tuple-element.20), channel_id=1, source_target_pairs={{1,2},{2,1},{5,6},{6,5},{17,18},{18,17},{21,22},{22,21}} | collective-permute-start | bytes 1572872 | tf_op jit(solution)/shard_map/ppermute | solution.py:23
  690.0 12.7 %collective-permute-start.126 = (bf16[256,1024]{1,0:T(8,128)(2,1)}, bf16[256,1024]{1,0:T(8,128)(2,1)S(1)}, u32[]{:S(2)}, u32[]{:S(2)}) collective-permute-start(bf16[256,1024]{1,0:T(8,128)(2,1)} %get-tuple-element.28), channel_id=1, source_target_pairs={{0,1},{1,0},{2,3},{3,2},{4,5},{5,4},{6,7},{7,6},{16,17},{17,16},{1... | collective-permute-start | bytes 1572872 | tf_op jit(solution)/shard_map/ppermute | solution.py:23
  703.4 12.7 %collective-permute-start.129 = (bf16[256,1024]{1,0:T(8,128)(2,1)}, bf16[256,1024]{1,0:T(8,128)(2,1)S(1)}, u32[]{:S(2)}, u32[]{:S(2)}) collective-permute-start(bf16[256,1024]{1,0:T(8,128)(2,1)} %collective-permute-done.128), channel_id=1, source_target_pairs={{1,0},{2,3},{5,4},{6,7},{17,16},{18,19},{21,20},{22,23}} | collective-permute-start | bytes 1572872 | tf_op jit(solution)/shard_map/ppermute | solution.py:23
  705.7 16.1 %collective-permute-start.64 = (bf16[256,1024]{1,0:T(8,128)(2,1)S(1)}, bf16[256,1024]{1,0:T(8,128)(2,1)S(1)}, u32[]{:S(2)}, u32[]{:S(2)}) collective-permute-start(bf16[256,1024]{1,0:T(8,128)(2,1)S(1)} %collective-permute-done.61), channel_id=1, source_target_pairs={{1,0},{2,3},{5,4},{6,7},{17,16},{18,19},{21,20},{22,23}} | collective-permute-start | bytes 1572872 | tf_op jit(solution)/shard_map/ppermute | solution.py:23
  707.0 20.4 %collective-permute-start.130 = (bf16[256,1024]{1,0:T(8,128)(2,1)S(1)}, bf16[256,1024]{1,0:T(8,128)(2,1)S(1)}, u32[]{:S(2)}, u32[]{:S(2)}) collective-permute-start(bf16[256,1024]{1,0:T(8,128)(2,1)S(1)} %collective-permute-done.127), channel_id=1, source_target_pairs={{1,0},{2,3},{5,4},{6,7},{17,16},{18,19},{21,20},{22,23}} | collective-permute-start | bytes 1572872 | tf_op jit(solution)/shard_map/ppermute | solution.py:23
  722.0 22.9 %collective-permute-start.65 = (bf16[256,4096]{1,0:T(8,128)(2,1)S(1)}, bf16[256,4096]{1,0:T(8,128)(2,1)}, u32[]{:S(2)}, u32[]{:S(2)}) collective-permute-start(bf16[256,4096]{1,0:T(8,128)(2,1)S(1)} %select_dynamic-update-slice_fusion.2), channel_id=1, source_target_pairs={{0,8},{1,9},{2,10},{3,11},{4,12},{5,13},{6,14},{7,15},{16,24},{17,... | collective-permute-start | bytes 6291464 | tf_op jit(solution)/shard_map/ppermute | solution.py:23
  728.4 18.3 %collective-permute-start.131 = (bf16[256,4096]{1,0:T(8,128)(2,1)}, bf16[256,4096]{1,0:T(8,128)(2,1)}, u32[]{:S(2)}, u32[]{:S(2)}) collective-permute-start(bf16[256,4096]{1,0:T(8,128)(2,1)} %select_dynamic-update-slice_fusion), channel_id=1, source_target_pairs={{0,8},{1,9},{2,10},{3,11},{4,12},{5,13},{6,14},{7,15},{16,24},{17,... | collective-permute-start | bytes 6291464 | tf_op jit(solution)/shard_map/ppermute | solution.py:23
  (107 other events, 1041.8 us)
